TPU v7x, 256 devices: a whole 4x4x8 slice. The times are simulated.
256 devices in a mesh: row: 8 (over x, core), col: 16 (over y, z_hi), rep: 2 (over z_lo).
Axes of the slice: x: 4, y: 4, z: 8 (z_hi: 4, z_lo: 2; z = z_hi * 2 + z_lo), core: 2. Of those that a mesh axis runs over, the one named last changes fastest.
Arguments:
- slab_half: float32 [2, 8192, 4096], P('rep', 'row', 'col'), may hold values from -6 to 6
- window_half: float32 [2, 4096, 8192], P('rep', 'row', 'col'), may hold values from -0.125 to 0.125
- slab_cols: int32 [64, 20], replicated, may hold values from 0 to 63, as said below
- window_cols: int32 [64, 20], replicated, may hold values from 0 to 63, as said below
Outputs:
- slab_square: float32 [8192, 8192], P(('row', 'rep'), 'col')
Inputs may be any that keep to these rules, and one draw needn't show every extreme that they name: `slab_cols`: each slab block row i lists 20 distinct block columns, all within 24 blocks of its centre, block column i; it lists the column exactly 24 blocks above the centre where that column exists, else the one exactly 24 blocks below where that exists. `window_cols`: each window block row k lists 20 distinct block columns, all within 24 blocks of column k; it lists column k + 24 where that column exists, else column k - 24 where that exists.
All inputs are finite; a program needn't handle non-finite values.
Results may differ from a plain program's by a relative error of at most 0.0001.
Values sent between devices are 32-bit elements; how exact they have to be, the bound alone decides.
A program may use at most 128 MiB of HBM per device.

v0:
```python
import jax
import jax.numpy as jnp
from jax import lax
from jax.sharding import PartitionSpec as P

BS = 128


def block_mask(columns, width):
    hit = columns[:, :, None] == jnp.arange(width, dtype=jnp.int32)[None, None, :]
    return jnp.any(hit, axis=1)


def expand(mask, size):
    filled = mask.astype(jnp.float32)
    return jnp.repeat(jnp.repeat(filled, size, axis=0), size, axis=1)


def product(left, right):
    return jnp.dot(left, right, precision=lax.Precision.HIGHEST, preferred_element_type=jnp.float32)


def body(slab_half, window_half, slab_cols, window_cols):
    row_index = lax.axis_index("row")
    col_index = lax.axis_index("col")
    rep_index = lax.axis_index("rep")
    window_width = window_cols.shape[0]
    half_blocks = window_width // lax.axis_size("rep")
    slab_blocks = half_blocks // lax.axis_size("col")
    window_blocks = half_blocks // lax.axis_size("row")
    slab_local = slab_half[0]
    window_local = window_half[0]
    row_blocks = slab_local.shape[0] // BS
    col_blocks = window_local.shape[1] // BS
    mask_a = block_mask(slab_cols, window_width)
    mask_b = block_mask(window_cols, window_width)
    half_start = rep_index * half_blocks
    row_start = row_index * row_blocks
    col_start = col_index * col_blocks
    mine_a = lax.dynamic_slice(
        mask_a, (row_start, half_start + col_index * slab_blocks), (row_blocks, slab_blocks)
    )
    mine_b = lax.dynamic_slice(
        mask_b, (half_start + row_index * window_blocks, col_start), (window_blocks, col_blocks)
    )
    slab_kept = slab_local * expand(mine_a, BS)
    window_kept = window_local * expand(mine_b, BS)
    slab_whole = lax.all_gather(slab_kept, "col", axis=1, tiled=True)
    partial_sum = product(slab_whole, lax.all_gather(window_kept, "row", axis=0, tiled=True))
    reduced = lax.psum_scatter(partial_sum, "rep", scatter_dimension=0, tiled=True)
    out_mask = expand(
        lax.dynamic_slice(mask_a, (row_start, col_start), (row_blocks, col_blocks)), BS
    )
    share = reduced.shape[0]
    out_local = lax.dynamic_slice_in_dim(out_mask, rep_index * share, share, 0)
    return reduced * out_local


def solution(mesh):
    in_specs = (P("rep", "row", "col"), P("rep", "row", "col"), P(), P())
    out_specs = P(("row", "rep"), "col")
    return jax.shard_map(body, mesh=mesh, in_specs=in_specs, out_specs=out_specs, check_vma=False)
```

profile of v0, /device:TPU:1, one launch (start us, length us, event | category | flops | bytes accessed | tf_op | source)
XLA Modules:
  0.0 355.2 jit_solution(626893484085413982)
XLA Ops:
  6.5 0.0 copy-start
  6.5 0.0 all-gather.5.cloned.1.call-start
  6.5 1.0 fusion.1
  7.6 0.1 dynamic-slice_convert_fusion.2
  7.7 0.6 broadcast_in_dim.25
  8.3 2.5 bitcast_multiply_fusion
  10.8 0.0 all-gather.5.cloned.1.call-update
  10.8 0.0 all-gather.3.cloned.1.call-start
  10.9 0.9 fusion
  11.8 0.1 dynamic-slice_convert_fusion.1
  11.9 1.2 broadcast_in_dim.23
  13.2 0.0 copy-done
  13.2 1.1 bitcast_multiply_fusion.1
  14.3 0.0 all-gather.3.cloned.1.call-update
  14.3 0.0 reduce-scatter.2.cloned.1.call-start
  14.4 53.0 %all-gather.5.cloned.1.call-done = f32[4096,512]{1,0:T(8,128)} async-done(((f32[512,512]{1,0:T(8,128)}), f32[4096,512]{1,0:T(8,128)}) %all-gather.5.cloned.1.call-update) | async-done | bytes 8388624 | tf_op jit(solution)/shard_map/all_gather | solution.py:49
  67.3 211.3 %all-gather.3.cloned.1.call-done = f32[1024,4096]{1,0:T(8,128)} async-done(((f32[1024,256]{1,0:T(8,128)}), f32[1024,4096]{1,0:T(8,128)}) %all-gather.3.cloned.1.call-update) | async-done | bytes 16777232 | tf_op jit(solution)/shard_map/all_gather | solution.py:48
  278.6 31.0 %fusion.2 = f32[1024,512]{1,0:T(8,128)} fusion(f32[1024,4096]{1,0:T(8,128)} %all-gather.3.cloned.1.call-done, f32[4096,512]{1,0:T(8,128)} %all-gather.5.cloned.1.call-done), kind=kOutput, calls=%fused_computation.11 | convolution fusion | flops 25769803776 | bytes 27262976 | tf_op jit(solution)/shard_map/dot_general | solution.py:20
  309.6 0.0 reduce-scatter.2.cloned.1.call-update
  309.7 0.1 dynamic-slice_convert_fusion
  309.8 1.2 broadcast_in_dim.27
  311.0 0.2 copy.13
  311.2 35.1 %reduce-scatter.2.cloned.1.call-done = f32[512,512]{1,0:T(8,128)} async-done(((f32[1024,512]{1,0:T(8,128)}), f32[512,512]{1,0:T(8,128)}) %reduce-scatter.2.cloned.1.call-update) | async-done | bytes 1048592 | tf_op jit(solution)/shard_map/reduce_scatter | solution.py:50
  346.3 2.4 dynamic-slice_multiply_fusion
  (3 shorter events, 0.1 us)
Async XLA Ops:
  6.5 6.6 %copy-start = (f32[1,1024,256]{2,1,0:T(8,128)S(1)}, f32[1,1024,256]{2,1,0:T(8,128)}, u32[]{:S(2)}) copy-start(f32[1,1024,256]{2,1,0:T(8,128)} %param.4) | copy-start | bytes 3145732
  6.5 60.8 %all-gather.5.cloned.1.call-start = ((), (), s32[]{:S(2)}) async-start(), calls=%async_computation.2 | async-start | bytes 9437184 | tf_op jit(solution)/shard_map/all_gather | solution.py:49
  10.8 267.8 %all-gather.3.cloned.1.call-start = ((), (), s32[]{:S(2)}) async-start(), calls=%async_computation.1 | async-start | bytes 17825792 | tf_op jit(solution)/shard_map/all_gather | solution.py:48
  14.3 332.0 %reduce-scatter.2.cloned.1.call-start = ((), (), s32[]{:S(2)}) async-start(), calls=%async_computation.3 | async-start | bytes 3145728 | tf_op jit(solution)/shard_map/reduce_scatter | solution.py:50
Sparse Core Ops, SparseCore 0:
  10.9 56.3 all-gather.4
  69.7 208.8 all-gather.2
  309.8 36.4 reduce-scatter.1
where the time goes:
time: 355 us
  waiting for transfers between devices  299 us (84%)
  matrix products  31 us (9%)
  between operations  13.2 us (4%)
  other arithmetic  8.21 us (2%)
    all_gather x1, waiting for transfers between devices, body(): slab_whole = lax.all_gather(slab_kept, 'col', axis=1, tiled=True)  211 us
    all_gather x1, waiting for transfers between devices, body(): lax.all_gather(window_kept, 'row', axis=0, tiled=True)  53 us
    reduce_scatter x1, waiting for transfers between devices, body(): lax.psum_scatter(partial_sum, 'rep', scatter_dimension=0, tiled=True)  35.1 us
    dot_general x1, matrix products, product(): jnp.dot(left, right, precision=lax.Precision.HIGHEST, preferred_element_t...  31 us
  transfers between devices with their start and end apart: 3, of which 3 were waited for; matrix products, arithmetic and copies ran while one was open for 1% of the time, Pallas kernels for 0%

commit v1 on v0

--- a/solution.py
+++ b/solution.py
@@ -45,7 +45,10 @@
     )
     slab_kept = slab_local * expand(mine_a, BS)
     window_kept = window_local * expand(mine_b, BS)
-    slab_whole = lax.all_gather(slab_kept, "col", axis=1, tiled=True)
+    count = lax.axis_size("col")
+    pieces = jnp.stack([slab_kept for _ in range(count)])
+    pieces = lax.all_to_all(pieces, "col", split_axis=0, concat_axis=0)
+    slab_whole = jnp.concatenate(pieces, axis=1)
     partial_sum = product(slab_whole, lax.all_gather(window_kept, "row", axis=0, tiled=True))
     reduced = lax.psum_scatter(partial_sum, "rep", scatter_dimension=0, tiled=True)
     out_mask = expand(

time: 355 us -> 508 us (1.43)
  waiting for transfers between devices: 299 us -> 432 us
  starting transfers between devices: 0.09 us -> 12.2 us
  local copies, waits for them, and re-layouts: 3.34 us -> 12.4 us
    all_to_all x0 -> x1, waiting for transfers between devices: none -> 312 us  [body(): pieces = lax.all_to_all(pieces, 'col', split_axis=0, concat_axis=0)]
    all_gather x1 -> x0, waiting for transfers between devices: 211 us -> none  [body(): slab_whole = lax.all_gather(slab_kept, 'col', axis=1, tiled=True)]
    reduce_scatter x1, waiting for transfers between devices: 35.1 us -> 66.3 us  [body(): lax.psum_scatter(partial_sum, 'rep', scatter_dimension=0, tiled=True)]
    all_to_all x0 -> x1, starting transfers between devices: none -> 11.9 us  [body(): pieces = lax.all_to_all(pieces, 'col', split_axis=0, concat_axis=0)]
    another operation x0 -> x2, local copies, waits for them, and re-layouts: none -> 8.18 us  [body(): pieces = jnp.stack([slab_kept for _ in range(count)])]
where the time goes in v1:
time: 508 us
  waiting for transfers between devices  432 us (85%)
  matrix products  31 us (6%)
  between operations  13.5 us (3%)
  local copies, waits for them, and re-layouts  12.4 us (2%)
  starting transfers between devices  12.2 us (2%)
  other arithmetic  6.47 us (1%)
    all_to_all x1, waiting for transfers between devices, body(): pieces = lax.all_to_all(pieces, 'col', split_axis=0, concat_axis=0)  312 us
    reduce_scatter x1, waiting for transfers between devices, body(): lax.psum_scatter(partial_sum, 'rep', scatter_dimension=0, tiled=True)  66.3 us
    all_gather x1, waiting for transfers between devices, body(): lax.all_gather(window_kept, 'row', axis=0, tiled=True)  54.4 us
    dot_general x1, matrix products, product(): jnp.dot(left, right, precision=lax.Precision.HIGHEST, preferred_element_t...  31 us
    all_to_all x1, starting transfers between devices, body(): pieces = lax.all_to_all(pieces, 'col', split_axis=0, concat_axis=0)  11.9 us
  transfers between devices with their start and end apart: 3, of which 3 were waited for; matrix products, arithmetic and copies ran while one was open for 1% of the time, Pallas kernels for 0%

profile of v1, /device:TPU:1, one launch (start us, length us, event | category | flops | bytes accessed | tf_op | source)
XLA Modules:
  0.0 507.9 jit_solution(10420544251533056419)
XLA Ops:
  6.5 0.9 fusion
  7.5 0.1 dynamic-slice_convert_fusion.1
  7.6 1.2 broadcast_in_dim.23
  8.9 0.8 reshape.29
  9.7 1.4 multiply_bitcast_fusion
  11.1 0.3 copy.10
  11.5 7.8 %stack.5 = f32[16,1024,256]{1,2,0:T(8,128)} broadcast(f32[1024,256]{0,1:T(8,128)S(1)} %copy.10), dimensions={1,2} | broadcast | bytes 17825792 | tf_op jit(solution)/shard_map/stack | solution.py:49
  19.3 11.9 %all-to-all-start = ((f32[16,1024,256]{1,2,0:T(8,128)}), f32[16,1024,256]{1,2,0:T(8,128)}, u32[]{:S(2)}, u32[]{:S(2)}) async-start(f32[16,1024,256]{1,2,0:T(8,128)} %stack.5), calls=%async_computation | async-start | bytes 33554432 | tf_op jit(solution)/shard_map/all_to_all | solution.py:50
  31.3 0.0 all-gather.2.cloned.1.call-start
  31.3 0.2 fusion.1
  31.6 0.1 dynamic-slice_convert_fusion.2
  31.7 0.6 broadcast_in_dim.25
  32.3 1.2 bitcast_multiply_fusion
  33.5 0.0 all-gather.2.cloned.1.call-update
  33.5 0.2 reduce-scatter.2.cloned.1.call-start
  33.7 54.4 %all-gather.2.cloned.1.call-done = f32[4096,512]{1,0:T(8,128)} async-done(((f32[512,512]{1,0:T(8,128)}), f32[4096,512]{1,0:T(8,128)}) %all-gather.2.cloned.1.call-update) | async-done | bytes 8388624 | tf_op jit(solution)/shard_map/all_gather | solution.py:52
  88.2 311.5 %all-to-all-done = f32[16,1024,256]{1,2,0:T(8,128)} async-done(((f32[16,1024,256]{1,2,0:T(8,128)}), f32[16,1024,256]{1,2,0:T(8,128)}, u32[]{:S(2)}, u32[]{:S(2)}) %all-to-all-start) | async-done | bytes 16777248 | tf_op jit(solution)/shard_map/all_to_all | solution.py:50
  399.7 31.0 %fusion.2 = f32[1024,512]{1,0:T(8,128)} fusion(f32[1024,4096]{0,1:T(8,128)} %bitcast.3, f32[4096,512]{1,0:T(8,128)} %all-gather.2.cloned.1.call-done), kind=kOutput, calls=%fused_computation.11 | convolution fusion | flops 25769803776 | bytes 27262976 | tf_op jit(solution)/shard_map/dot_general | solution.py:20
  430.7 0.0 reduce-scatter.2.cloned.1.call-update
  430.8 0.1 dynamic-slice_convert_fusion
  430.9 1.2 broadcast_in_dim.27
  432.1 0.2 copy.15
  432.3 66.3 %reduce-scatter.2.cloned.1.call-done = f32[512,512]{1,0:T(8,128)} async-done(((f32[1024,512]{1,0:T(8,128)}), f32[512,512]{1,0:T(8,128)}) %reduce-scatter.2.cloned.1.call-update) | async-done | bytes 1048592 | tf_op jit(solution)/shard_map/reduce_scatter | solution.py:53
  498.6 2.4 dynamic-slice_multiply_fusion
  (7 shorter events, 0.1 us)
Async XLA Ops:
  19.3 12.0 %copy-start.1 = (s32[64,20]{0,1:T(8,128)S(1)}, s32[64,20]{0,1:T(8,128)}, u32[]{:S(2)}) copy-start(s32[64,20]{0,1:T(8,128)} %param.7) | copy-start | bytes 15364
  19.3 13.0 %copy-start = (f32[1,512,512]{2,1,0:T(8,128)S(1)}, f32[1,512,512]{2,1,0:T(8,128)}, u32[]{:S(2)}) copy-start(f32[1,512,512]{2,1,0:T(8,128)} %param.5) | copy-start | bytes 3145732
  19.3 380.4 %all-to-all-start = ((f32[16,1024,256]{1,2,0:T(8,128)}), f32[16,1024,256]{1,2,0:T(8,128)}, u32[]{:S(2)}, u32[]{:S(2)}) async-start(f32[16,1024,256]{1,2,0:T(8,128)} %stack.5), calls=%async_computation | async-start | bytes 33554432 | tf_op jit(solution)/shard_map/all_to_all | solution.py:50
  31.3 56.9 %all-gather.2.cloned.1.call-start = ((), (), s32[]{:S(2)}) async-start(), calls=%async_computation.2 | async-start | bytes 9437184 | tf_op jit(solution)/shard_map/all_gather | solution.py:52
  33.5 465.2 %reduce-scatter.2.cloned.1.call-start = ((), (), s32[]{:S(2)}) async-start(), calls=%async_computation.3 | async-start | bytes 3145728 | tf_op jit(solution)/shard_map/reduce_scatter | solution.py:53
Sparse Core Ops, SparseCore 0:
  33.9 54.1 all-gather.1
  430.9 67.7 reduce-scatter.1
